TPU v7x, 512 devices: a whole 4x8x8 slice. The times are simulated.
512 devices in a mesh: dp: 4 (over x), seq: 16 (over z, core), tensor: 8 (over y).
Axes of the slice: x: 4, y: 8, z: 8, core: 2. Of those that a mesh axis runs over, the one named last changes fastest.
Arguments:
- hidden: bfloat16 [8192, 8192], P(('dp', 'seq'), 'tensor'), may hold values from -6 to 6
- queries: bfloat16 [8192, 8192], P(('dp', 'seq'), 'tensor'), may hold values from -14 to 14
- kv_weight: bfloat16 [8192, 2048], P('seq', 'tensor'), may hold values from -0.0625 to 0.0625
- parents: int32 [4, 16], P('dp'), may hold values from -1 to 14, as said below
- out_grad: bfloat16 [8192, 8192], P(('dp', 'seq'), 'tensor'), may hold values from -6 to 6
Outputs:
- attended: bfloat16 [8192, 8192], P(('dp', 'seq'), 'tensor')
- query_grad: float32 [8192, 8192], P(('dp', 'seq'), 'tensor')
- weight_grad: float32 [8192, 2048], P('seq', 'tensor')
Inputs may be any that keep to these rules, and one draw needn't show every extreme that they name: parents[g, n] is -1 where node block n begins a new tree of group g (always for n = 0), else an earlier node block of the same group; the last node block of every group has parent 16 - 2.
All inputs are finite; a program needn't handle non-finite values.
Results may differ from a plain program's by a relative error of at most 0.012.
The roundings to bfloat16 on the way count: a program that leaves them out, or rounds other values in their place, can miss the bound.
Values may be sent and summed in bfloat16 or wider, within the bound.
No kernel may reach another device: no remote copies, remote signals or barrier semaphores. Data moves between devices by JAX's collectives and lax.ppermute only.
A program may use at most 64 MiB of HBM per device.

v0:
```python
import math
import jax
import jax.numpy as jnp
from jax import lax
from jax.sharding import PartitionSpec as P

HD = 128


def attend_block(query_blk, grad_blk, keys_head, values_head, visible):
    inv_root = 1.0 / math.sqrt(query_blk.shape[-1])
    scores = (
        jnp.einsum("thd,jd->htj", query_blk, keys_head, preferred_element_type=jnp.float32)
        * inv_root
    )
    scores = jnp.where(visible[None], scores, -jnp.inf)
    row_top = jnp.max(scores, axis=-1, keepdims=True)
    expons = jnp.exp(scores - row_top)
    probs_f = expons / jnp.sum(expons, axis=-1, keepdims=True)
    weights = probs_f.astype(jnp.bfloat16)
    mixed_f = jnp.einsum("htj,jd->thd", weights, values_head, preferred_element_type=jnp.float32)
    prob_grad = jnp.einsum("thd,jd->htj", grad_blk, values_head, preferred_element_type=jnp.float32)
    inner_sum = jnp.transpose(jnp.sum(grad_blk.astype(jnp.float32) * mixed_f, axis=-1), (1, 0))
    score_grad = (probs_f * (prob_grad - inner_sum[:, :, None]) * inv_root).astype(jnp.bfloat16)
    query_grad = jnp.einsum(
        "htj,jd->thd", score_grad, keys_head, preferred_element_type=jnp.float32
    )
    key_grad = jnp.einsum("htj,thd->jd", score_grad, query_blk, preferred_element_type=jnp.float32)
    value_grad = jnp.einsum("htj,thd->jd", weights, grad_blk, preferred_element_type=jnp.float32)
    return (mixed_f.astype(jnp.bfloat16), query_grad, key_grad, value_grad)


def per_device(hidden, queries, kv_weight, parents, out_grad):
    tok_rows = queries.shape[0]
    head_size = HD
    kv_local = kv_weight.shape[1] // (2 * head_size)
    heads_local = queries.shape[1] // head_size
    heads_per = heads_local // kv_local
    block_heads = max(1, min(heads_per, 512 // tok_rows))
    block_count = heads_per // block_heads
    node_count = lax.axis_size("seq")
    my_node = lax.axis_index("seq")
    group_rows = tok_rows * node_count
    whole_rows = lax.all_gather(hidden, "tensor", axis=1, tiled=True)
    traded = lax.all_to_all(whole_rows, "seq", split_axis=1, concat_axis=0, tiled=True)
    partial_kv = jnp.dot(traded, kv_weight, preferred_element_type=jnp.float32)
    kv_all = lax.psum(partial_kv, "seq").astype(jnp.bfloat16)
    parent_list = parents[0]
    node_ids = jnp.arange(node_count, dtype=jnp.int32)

    def follow(step_index, state_pair):
        current, marked = state_pair
        marked = jnp.maximum(marked, (node_ids == current).astype(jnp.int32))
        current = jnp.where(current >= 0, parent_list[jnp.maximum(current, 0)], -1)
        return (current, marked)

    start_pair = (parent_list[my_node], jnp.zeros((node_count,), jnp.int32))
    final_pair = lax.fori_loop(0, node_count, follow, start_pair)
    key_above = jnp.broadcast_to(final_pair[1][:, None] > 0, (node_count, tok_rows)).reshape(
        group_rows
    )
    key_node = jnp.arange(group_rows, dtype=jnp.int32) // tok_rows
    key_pos = jnp.arange(group_rows, dtype=jnp.int32) % tok_rows
    query_pos = jnp.arange(tok_rows, dtype=jnp.int32)
    visible = key_above[None, :] | (key_node == my_node)[None, :] & (
        key_pos[None, :] <= query_pos[:, None]
    )
    kv_heads = kv_all.reshape(group_rows, kv_local, 2, head_size).transpose(1, 0, 2, 3)
    query_split = queries.reshape(
        tok_rows, kv_local, block_count, block_heads, head_size
    ).transpose(1, 2, 0, 3, 4)
    grad_split = out_grad.reshape(
        tok_rows, kv_local, block_count, block_heads, head_size
    ).transpose(1, 2, 0, 3, 4)

    def per_head(packed):
        query_head, grad_head, head_kv = packed
        keys_head = head_kv[:, 0, :]
        values_head = head_kv[:, 1, :]

        def per_part(running, block_pair):
            mixed_blk, qgrad_blk, key_grad, value_grad = attend_block(
                block_pair[0], block_pair[1], keys_head, values_head, visible
            )
            return ((running[0] + key_grad, running[1] + value_grad), (mixed_blk, qgrad_blk))

        zero_grad = jnp.zeros((group_rows, head_size), jnp.float32)
        sums_pair, outputs = lax.scan(per_part, (zero_grad, zero_grad), (query_head, grad_head))
        return (outputs[0], outputs[1], jnp.stack([sums_pair[0], sums_pair[1]], axis=1))

    mixed_all, qgrad_all, kv_terms = lax.map(per_head, (query_split, grad_split, kv_heads))
    attended = mixed_all.transpose(2, 0, 1, 3, 4).reshape(tok_rows, heads_local * head_size)
    query_grad = qgrad_all.transpose(2, 0, 1, 3, 4).reshape(tok_rows, heads_local * head_size)
    kv_terms = kv_terms.transpose(1, 0, 2, 3).reshape(group_rows, kv_local * 2 * head_size)
    kv_grads = lax.psum(kv_terms.astype(jnp.bfloat16), "seq")
    local_weight = lax.dot_general(
        traded, kv_grads, (((0,), (0,)), ((), ())), preferred_element_type=jnp.float32
    )
    weight_grad = lax.psum(local_weight * (1.0 / (lax.axis_size("dp") * node_count)), "dp")
    return (attended, query_grad, weight_grad)


def solution(mesh):
    placed = (
        P(("dp", "seq"), "tensor"),
        P(("dp", "seq"), "tensor"),
        P("seq", "tensor"),
        P("dp", None),
        P(("dp", "seq"), "tensor"),
    )
    return jax.shard_map(
        per_device,
        mesh=mesh,
        in_specs=placed,
        out_specs=(P(("dp", "seq"), "tensor"), P(("dp", "seq"), "tensor"), P("seq", "tensor")),
        check_vma=False,
    )
```

profile of v0, /device:TPU:8, one launch (start us, length us, event | category | flops | bytes accessed | tf_op | source)
XLA Modules:
  0.0 414.3 jit_solution(17990220807136559389)
XLA Ops:
  13.4 45.1 %all-gather.2.cloned.1.call-done = bf16[128,8192]{0,1:T(8,128)(2,1)} async-done(((bf16[128,1024]{0,1:T(8,128)(2,1)}), bf16[128,8192]{0,1:T(8,128)(2,1)}) %all-gather.2.cloned.1.call-update) | async-done | bytes 2097168 | tf_op jit(solution)/shard_map/all_gather | solution.py:44
  58.4 7.5 %all-to-all-start = ((bf16[128,16,512]{0,2,1:T(8,128)(2,1)}), bf16[128,16,512]{0,2,1:T(8,128)(2,1)S(1)}, u32[]{:S(2)}, u32[]{:S(2)}) async-start(bf16[128,16,512]{0,2,1:T(8,128)(2,1)} %bitcast.163), calls=%async_computation | async-start | bytes 4194304 | tf_op jit(solution)/shard_map/all_to_all | solution.py:45
  66.0 40.3 %while.42 = (s32[]{:T(128)}, s32[]{:T(128)}, s32[16]{0:T(128)S(1)}, s32[16]{0:T(128)S(1)}, s32[]{:T(128)}, /*index=5*/s32[]{:T(128)}, s32[]{:T(128)}) while((s32[]{:T(128)}, s32[]{:T(128)}, s32[16]{0:T(128)S(1)}, s32[16]{0:T(128)S(1)}, s32[]{:T(128)}, /*index=5*/s32[]{:T(128)}, s32[]{:T(128)}) %tuple.73), condition=%wide.region_2.3_spmd.clone, body=%wide.region_1.2_spmd.clone.sunk | while | flops 70 | bytes 273 | solution.py:58
  106.4 8.8 %all-to-all-done = bf16[128,16,512]{0,2,1:T(8,128)(2,1)S(1)} async-done(((bf16[128,16,512]{0,2,1:T(8,128)(2,1)}), bf16[128,16,512]{0,2,1:T(8,128)(2,1)S(1)}, u32[]{:S(2)}, u32[]{:S(2)}) %all-to-all-start) | async-done | bytes 2097184 | tf_op jit(solution)/shard_map/all_to_all | solution.py:45
  116.5 2.9 copy.38
  119.4 2.0 fusion.48
  121.4 60.2 %all-reduce.7 = bf16[2048,256]{1,0:T(8,128)(2,1)} all-reduce(f32[2048,256]{1,0:T(8,128)} %fusion.48), channel_id=1, replica_groups=mesh['dp'=4,'seq'=16,'tensor'=8] {'seq'}, use_global_device_ids=true, to_apply=%region_0.0 | all-reduce | flops 524288 | bytes 3145728 | tf_op jit(solution)/shard_map/psum | solution.py:47
  181.6 2.2 squeeze.41
  183.8 3.2 fusion.47
  188.9 39.9 %while.43 = (s32[]{:T(128)}, f32[2048,128]{1,0:T(8,128)}, f32[2048,128]{1,0:T(8,128)}, bf16[2,128,4,128]{3,1,2,0:T(8,128)(2,1)}, f32[2,128,4,128]{3,1,2,0:T(8,12...) while((s32[]{:T(128)}, f32[2048,128]{1,0:T(8,128)}, ...), condition=%wide.region_7.8_spmd.clone, body=%wide.region_3.7_spmd.clone.sunk | while | flops 1626342912 | bytes 79985504 | solution.py:88
  189.8 1.9 fusion.91
  191.7 1.9 copy-done.2
  195.4 1.8 multiply_reduce_fusion.2
  197.2 4.5 %fusion.93 = bf16[4,128,2048]{2,1,0:T(8,128)(2,1)} fusion(f32[4,128]{1,0:T(4,128)S(1)} %bitcast.169, f32[4,128,2048]{2,1,0:T(8,128)} %copy-done.2, f32[4,128]{1,0:T(4,128)} %copy-done.11, bf16[2048,128]{0,1:T(8,128)(2,1)} %get-tuple-element.411, bf16[1,128,4,128]{1,3,2,0:T(8,128)(2,1)S(1)} %constant_dynamic-slice_fusion.3), kind=kOutput, calls=%fused_computation.9.clone.1 | convolution fusion | flops 273678336 | bytes 6950912 | tf_op jit(solution)/shard_map/while/body/eval_jaxpr/while/body/eval_jaxpr/thd,jd->htj/dot_general | solution.py:22
  201.8 3.5 fusion.94
  209.7 1.9 fusion.91
  211.6 1.9 copy-done.2
  215.2 1.8 multiply_reduce_fusion.2
  217.1 4.5 %fusion.93 = bf16[4,128,2048]{2,1,0:T(8,128)(2,1)} fusion(f32[4,128]{1,0:T(4,128)S(1)} %bitcast.169, f32[4,128,2048]{2,1,0:T(8,128)} %copy-done.2, f32[4,128]{1,0:T(4,128)} %copy-done.11, bf16[2048,128]{0,1:T(8,128)(2,1)} %get-tuple-element.411, bf16[1,128,4,128]{1,3,2,0:T(8,128)(2,1)S(1)} %constant_dynamic-slice_fusion.3), kind=kOutput, calls=%fused_computation.9.clone.1 | convolution fusion | flops 273678336 | bytes 6950912 | tf_op jit(solution)/shard_map/while/body/eval_jaxpr/while/body/eval_jaxpr/thd,jd->htj/dot_general | solution.py:22
  221.6 3.8 fusion.94
  233.0 116.3 %all-reduce.4.cloned.1.call-done = bf16[2048,256]{0,1:T(8,128)(2,1)} async-done(((bf16[2048,256]{0,1:T(8,128)(2,1)}), bf16[2048,256]{0,1:T(8,128)(2,1)}) %all-reduce.4.cloned.1.call-update) | async-done | bytes 1048592 | tf_op jit(solution)/shard_map/psum | solution.py:95
  349.3 2.7 fusion.37
  355.5 50.2 %all-reduce.6.cloned.1.call-done = f32[512,256]{0,1:T(8,128)} async-done(((f32[512,256]{0,1:T(8,128)}), f32[512,256]{0,1:T(8,128)}) %all-reduce.6.cloned.1.call-update) | async-done | bytes 524304 | tf_op jit(solution)/shard_map/psum | solution.py:99
  405.7 2.0 copy.48
  (114 shorter events, 38.6 us)
Async XLA Ops:
  7.2 112.2 %copy-start = (bf16[512,256]{1,0:T(8,128)(2,1)S(1)}, bf16[512,256]{1,0:T(8,128)(2,1)}, u32[]{:S(2)}) copy-start(bf16[512,256]{1,0:T(8,128)(2,1)} %param.11) | copy-start | bytes 786436
  7.2 58.8 %copy-start.12 = (s32[1,16]{1,0:T(1,128)S(1)}, s32[1,16]{1,0:T(1,128)}, u32[]{:S(2)}) copy-start(s32[1,16]{1,0:T(1,128)} %param.12) | copy-start | bytes 196
  7.2 51.3 %all-gather.2.cloned.1.call-start = ((), (), s32[]{:S(2)}) async-start(), calls=%async_computation.1 | async-start | bytes 2359296 | tf_op jit(solution)/shard_map/all_gather | solution.py:44
  58.4 56.7 %all-to-all-start = ((bf16[128,16,512]{0,2,1:T(8,128)(2,1)}), bf16[128,16,512]{0,2,1:T(8,128)(2,1)S(1)}, u32[]{:S(2)}, u32[]{:S(2)}) async-start(bf16[128,16,512]{0,2,1:T(8,128)(2,1)} %bitcast.163), calls=%async_computation | async-start | bytes 4194304 | tf_op jit(solution)/shard_map/all_to_all | solution.py:45
  65.9 283.4 %all-reduce.4.cloned.1.call-start = ((), (), s32[]{:S(2)}) async-start(), calls=%async_computation.2 | async-start | bytes 2097152 | tf_op jit(solution)/shard_map/psum | solution.py:95
  115.2 1.3 copy-start.7
  119.4 62.2 %copy-start.5 = (bf16[16,128,512]{2,1,0:T(8,128)(2,1)}, bf16[16,128,512]{2,1,0:T(8,128)(2,1)S(1)}, u32[]{:S(2)}) copy-start(bf16[16,128,512]{2,1,0:T(8,128)(2,1)S(1)} %copy.38) | copy-start | bytes 6291460
  191.7 2.0 copy-start.2
  191.7 2.6 copy-start.11
  201.8 3.6 copy-start.1
  201.8 3.6 copy-start.8
  201.8 4.3 %copy-start.3 = (f32[2048,128]{1,0:T(8,128)S(1)}, f32[2048,128]{1,0:T(8,128)}, u32[]{:S(2)}) copy-start(f32[2048,128]{1,0:T(8,128)} %get-tuple-element.391) | copy-start | bytes 3145732 | tf_op jit(solution)/shard_map/while/body/eval_jaxpr/while
  206.0 2.0 copy-start.9
  207.1 1.0 copy-start.4
  211.5 2.0 copy-start.2
  211.5 2.6 copy-start.11
  221.6 3.8 copy-start.1
  221.6 3.8 copy-start.8
  221.6 4.5 %copy-start.3 = (f32[2048,128]{1,0:T(8,128)S(1)}, f32[2048,128]{1,0:T(8,128)}, u32[]{:S(2)}) copy-start(f32[2048,128]{1,0:T(8,128)} %get-tuple-element.391) | copy-start | bytes 3145732 | tf_op jit(solution)/shard_map/while/body/eval_jaxpr/while
  226.1 2.0 copy-start.9
  227.2 1.0 copy-start.4
  228.8 120.5 %copy-start.6 = (bf16[16,128,512]{2,1,0:T(8,128)(2,1)S(1)}, bf16[16,128,512]{2,1,0:T(8,128)(2,1)}, u32[]{:S(2)}) copy-start(bf16[16,128,512]{2,1,0:T(8,128)(2,1)} %copy-done.5) | copy-start | bytes 6291460
  232.9 119.2 %copy-start.10 = (f32[2,128,4,128]{3,1,2,0:T(8,128)S(1)}, f32[2,128,4,128]{3,1,2,0:T(8,128)}, u32[]{:S(2)}) copy-start(f32[2,128,4,128]{3,1,2,0:T(8,128)} %get-tuple-element.111) | copy-start | bytes 1572868
  232.9 172.8 %all-reduce.6.cloned.1.call-start = ((), (), s32[]{:S(2)}) async-start(), calls=%async_computation.3 | async-start | bytes 1048576 | tf_op jit(solution)/shard_map/psum | solution.py:99
Sparse Core Ops, SparseCore 0:
  10.7 47.7 all-gather.1
  233.1 116.2 all-reduce.3
  352.2 53.4 all-reduce.5
where the time goes:
time: 415 us; the launch traced here: 414 us
  waiting for transfers between devices  220 us (53%)
  blocking collectives  60.2 us (15%)
  local copies, waits for them, and re-layouts  44.7 us (11%)
  loops' own time  30.9 us (7%)
  matrix products  29.8 us (7%)
  between operations  13.9 us (3%)
  starting transfers between devices  7.6 us (2%)
  other arithmetic  6.75 us (2%)
    psum x1, waiting for transfers between devices, per_device(): kv_grads = lax.psum(kv_terms.astype(jnp.bfloat16), 'seq')  116 us
    psum x1, blocking collectives, per_device(): kv_all = lax.psum(partial_kv, 'seq').astype(jnp.bfloat16)  60.2 us
    psum x1, waiting for transfers between devices, per_device(): lax.psum(local_weight * (1.0 / (lax.axis_size('dp') * node_count)), 'dp')  50.2 us
    all_gather x1, waiting for transfers between devices, per_device(): whole_rows = lax.all_gather(hidden, 'tensor', axis=1, tiled=True)  45.1 us
    another operation x1, loops' own time, per_device(): final_pair = lax.fori_loop(0, node_count, follow, start_pair)  30.7 us
    unnamed x18, local copies, waits for them, and re-layouts  10 us
    dynamic_slice x16, local copies, waits for them, and re-layouts, follow(): current = jnp.where(current >= 0, parent_list[jnp.maximum(current, 0)], -1)  9.39 us
    dot_general x2, matrix products, attend_block(): jnp.einsum('thd,jd->htj', grad_blk, values_head, preferred_element_type=j...  9.07 us
  transfers between devices with their start and end apart: 4, of which 4 were waited for; matrix products, arithmetic and copies ran while one was open for 4% of the time, Pallas kernels for 0%

commit v1 on v0

--- a/solution.py
+++ b/solution.py
@@ -5,6 +5,11 @@
 from jax.sharding import PartitionSpec as P
 
 HD = 128
+
+
+def summed_here(value, axis):
+    terms = lax.all_gather(value, axis)
+    return jnp.sum(terms, axis=0)
 
 
 def attend_block(query_blk, grad_blk, keys_head, values_head, visible):
@@ -96,7 +101,7 @@
     local_weight = lax.dot_general(
         traded, kv_grads, (((0,), (0,)), ((), ())), preferred_element_type=jnp.float32
     )
-    weight_grad = lax.psum(local_weight * (1.0 / (lax.axis_size("dp") * node_count)), "dp")
+    weight_grad = summed_here(local_weight * (1.0 / (lax.axis_size("dp") * node_count)), "dp")
     return (attended, query_grad, weight_grad)
 
 

time: 415 us -> 401 us (0.966)
  the two profiles are of different devices: /device:TPU:8 before, /device:TPU:1 now
where the time goes in v1:
time: 401 us; the launch traced here: 400 us
  waiting for transfers between devices  202 us (50%)
  blocking collectives  56.6 us (14%)
  local copies, waits for them, and re-layouts  46.3 us (12%)
  loops' own time  30.9 us (8%)
  matrix products  29.8 us (7%)
  between operations  13.9 us (3%)
  starting transfers between devices  12.5 us (3%)
  other arithmetic  7.99 us (2%)
    psum x1, waiting for transfers between devices, per_device(): kv_grads = lax.psum(kv_terms.astype(jnp.bfloat16), 'seq')  119 us
    psum x1, blocking collectives, per_device(): kv_all = lax.psum(partial_kv, 'seq').astype(jnp.bfloat16)  56.6 us
    all_gather x1, waiting for transfers between devices, per_device(): whole_rows = lax.all_gather(hidden, 'tensor', axis=1, tiled=True)  42 us
    all_gather x1, waiting for transfers between devices, summed_here(): terms = lax.all_gather(value, axis)  32.5 us
    another operation x1, loops' own time, per_device(): final_pair = lax.fori_loop(0, node_count, follow, start_pair)  30.7 us
    all_to_all x1, starting transfers between devices, per_device(): lax.all_to_all(whole_rows, 'seq', split_axis=1, concat_axis=0, tiled=True)  12.2 us
    dynamic_slice x16, local copies, waits for them, and re-layouts, follow(): current = jnp.where(current >= 0, parent_list[jnp.maximum(current, 0)], -1)  9.39 us
    dot_general x2, matrix products, attend_block(): jnp.einsum('thd,jd->htj', grad_blk, values_head, preferred_element_type=j...  9.07 us
  transfers between devices with their start and end apart: 4, of which 4 were waited for; matrix products, arithmetic and copies ran while one was open for 4% of the time, Pallas kernels for 0%

profile of v1, /device:TPU:1, one launch (start us, length us, event | category | flops | bytes accessed | tf_op | source)
XLA Modules:
  0.0 400.3 jit_solution(12857773980662832948)
XLA Ops:
  13.4 42.0 %all-gather.4.cloned.1.call-done = bf16[128,8192]{0,1:T(8,128)(2,1)} async-done(((bf16[128,1024]{0,1:T(8,128)(2,1)}), bf16[128,8192]{0,1:T(8,128)(2,1)}) %all-gather.4.cloned.1.call-update) | async-done | bytes 2097168 | tf_op jit(solution)/shard_map/all_gather | solution.py:49
  55.4 12.2 %all-to-all-start = ((bf16[128,16,512]{0,2,1:T(8,128)(2,1)}), bf16[128,16,512]{0,2,1:T(8,128)(2,1)S(1)}, u32[]{:S(2)}, u32[]{:S(2)}) async-start(bf16[128,16,512]{0,2,1:T(8,128)(2,1)} %bitcast.165), calls=%async_computation | async-start | bytes 4194304 | tf_op jit(solution)/shard_map/all_to_all | solution.py:50
  67.6 40.3 %while.42 = (s32[]{:T(128)}, s32[]{:T(128)}, s32[16]{0:T(128)S(1)}, s32[16]{0:T(128)S(1)}, s32[]{:T(128)}, /*index=5*/s32[]{:T(128)}, s32[]{:T(128)}) while((s32[]{:T(128)}, s32[]{:T(128)}, s32[16]{0:T(128)S(1)}, s32[16]{0:T(128)S(1)}, s32[]{:T(128)}, /*index=5*/s32[]{:T(128)}, s32[]{:T(128)}) %tuple.72), condition=%wide.region_2.3_spmd.clone, body=%wide.region_1.2_spmd.clone.sunk | while | flops 70 | bytes 273 | solution.py:63
  108.0 8.6 %all-to-all-done = bf16[128,16,512]{0,2,1:T(8,128)(2,1)S(1)} async-done(((bf16[128,16,512]{0,2,1:T(8,128)(2,1)}), bf16[128,16,512]{0,2,1:T(8,128)(2,1)S(1)}, u32[]{:S(2)}, u32[]{:S(2)}) %all-to-all-start) | async-done | bytes 2097184 | tf_op jit(solution)/shard_map/all_to_all | solution.py:50
  118.0 2.9 copy.52
  120.8 2.0 fusion.48
  122.9 56.6 %all-reduce.4 = bf16[2048,256]{1,0:T(8,128)(2,1)} all-reduce(f32[2048,256]{1,0:T(8,128)} %fusion.48), channel_id=1, replica_groups=mesh['dp'=4,'seq'=16,'tensor'=8] {'seq'}, use_global_device_ids=true, to_apply=%region_0.0 | all-reduce | flops 524288 | bytes 3145728 | tf_op jit(solution)/shard_map/psum | solution.py:52
  179.4 2.2 squeeze.41
  181.6 3.2 fusion.47
  186.7 39.9 %while.43 = (s32[]{:T(128)}, f32[2048,128]{1,0:T(8,128)}, f32[2048,128]{1,0:T(8,128)}, bf16[2,128,4,128]{3,1,2,0:T(8,128)(2,1)}, f32[2,128,4,128]{3,1,2,0:T(8,12...) while((s32[]{:T(128)}, f32[2048,128]{1,0:T(8,128)}, ...), condition=%wide.region_7.8_spmd.clone, body=%wide.region_3.7_spmd.clone.sunk | while | flops 1626342912 | bytes 79985504 | solution.py:93
  187.7 1.9 fusion.91
  189.6 1.9 copy-done.2
  193.2 1.8 multiply_reduce_fusion.2
  195.1 4.5 %fusion.93 = bf16[4,128,2048]{2,1,0:T(8,128)(2,1)} fusion(f32[4,128]{1,0:T(4,128)S(1)} %bitcast.171, f32[4,128,2048]{2,1,0:T(8,128)} %copy-done.2, f32[4,128]{1,0:T(4,128)} %copy-done.11, bf16[2048,128]{0,1:T(8,128)(2,1)} %get-tuple-element.417, bf16[1,128,4,128]{1,3,2,0:T(8,128)(2,1)S(1)} %constant_dynamic-slice_fusion.3), kind=kOutput, calls=%fused_computation.9.clone.1 | convolution fusion | flops 273678336 | bytes 6950912 | tf_op jit(solution)/shard_map/while/body/eval_jaxpr/while/body/eval_jaxpr/thd,jd->htj/dot_general | solution.py:27
  199.6 3.5 fusion.94
  207.5 1.9 fusion.91
  209.4 1.9 copy-done.2
  213.1 1.8 multiply_reduce_fusion.2
  214.9 4.5 %fusion.93 = bf16[4,128,2048]{2,1,0:T(8,128)(2,1)} fusion(f32[4,128]{1,0:T(4,128)S(1)} %bitcast.171, f32[4,128,2048]{2,1,0:T(8,128)} %copy-done.2, f32[4,128]{1,0:T(4,128)} %copy-done.11, bf16[2048,128]{0,1:T(8,128)(2,1)} %get-tuple-element.417, bf16[1,128,4,128]{1,3,2,0:T(8,128)(2,1)S(1)} %constant_dynamic-slice_fusion.3), kind=kOutput, calls=%fused_computation.9.clone.1 | convolution fusion | flops 273678336 | bytes 6950912 | tf_op jit(solution)/shard_map/while/body/eval_jaxpr/while/body/eval_jaxpr/thd,jd->htj/dot_general | solution.py:27
  219.4 3.8 fusion.94
  231.0 119.1 %all-reduce.3.cloned.1.call-done = bf16[2048,256]{0,1:T(8,128)(2,1)} async-done(((bf16[2048,256]{0,1:T(8,128)(2,1)}), bf16[2048,256]{0,1:T(8,128)(2,1)}) %all-reduce.3.cloned.1.call-update) | async-done | bytes 1048592 | tf_op jit(solution)/shard_map/psum | solution.py:100
  350.1 2.7 fusion.37
  356.3 32.5 %all-gather.6.cloned.1.call-done = f32[2048,256]{0,1:T(8,128)} async-done(((f32[512,256]{0,1:T(8,128)}), f32[2048,256]{0,1:T(8,128)}) %all-gather.6.cloned.1.call-update) | async-done | bytes 2097168 | tf_op jit(solution)/shard_map/all_gather | solution.py:11
  388.8 2.7 reshape.60
  (116 shorter events, 41.0 us)
Async XLA Ops:
  7.2 113.7 %copy-start = (bf16[512,256]{1,0:T(8,128)(2,1)S(1)}, bf16[512,256]{1,0:T(8,128)(2,1)}, u32[]{:S(2)}) copy-start(bf16[512,256]{1,0:T(8,128)(2,1)} %param.11) | copy-start | bytes 786436
  7.2 60.4 %copy-start.12 = (s32[1,16]{1,0:T(1,128)S(1)}, s32[1,16]{1,0:T(1,128)}, u32[]{:S(2)}) copy-start(s32[1,16]{1,0:T(1,128)} %param.12) | copy-start | bytes 196
  7.2 48.2 %all-gather.4.cloned.1.call-start = ((), (), s32[]{:S(2)}) async-start(), calls=%async_computation.1 | async-start | bytes 2359296 | tf_op jit(solution)/shard_map/all_gather | solution.py:49
  55.4 61.3 %all-to-all-start = ((bf16[128,16,512]{0,2,1:T(8,128)(2,1)}), bf16[128,16,512]{0,2,1:T(8,128)(2,1)S(1)}, u32[]{:S(2)}, u32[]{:S(2)}) async-start(bf16[128,16,512]{0,2,1:T(8,128)(2,1)} %bitcast.165), calls=%async_computation | async-start | bytes 4194304 | tf_op jit(solution)/shard_map/all_to_all | solution.py:50
  67.6 282.6 %all-reduce.3.cloned.1.call-start = ((), (), s32[]{:S(2)}) async-start(), calls=%async_computation.2 | async-start | bytes 2097152 | tf_op jit(solution)/shard_map/psum | solution.py:100
  116.6 1.3 copy-start.7
  120.8 58.6 %copy-start.5 = (bf16[16,128,512]{2,1,0:T(8,128)(2,1)}, bf16[16,128,512]{2,1,0:T(8,128)(2,1)S(1)}, u32[]{:S(2)}) copy-start(bf16[16,128,512]{2,1,0:T(8,128)(2,1)S(1)} %copy.52) | copy-start | bytes 6291460
  189.5 2.0 copy-start.2
  189.5 2.6 copy-start.11
  199.6 3.6 copy-start.1
  199.6 3.6 copy-start.8
  199.6 4.3 %copy-start.3 = (f32[2048,128]{1,0:T(8,128)S(1)}, f32[2048,128]{1,0:T(8,128)}, u32[]{:S(2)}) copy-start(f32[2048,128]{1,0:T(8,128)} %get-tuple-element.397) | copy-start | bytes 3145732 | tf_op jit(solution)/shard_map/while/body/eval_jaxpr/while
  203.9 2.0 copy-start.9
  204.9 1.0 copy-start.4
  209.4 2.0 copy-start.2
  209.4 2.6 copy-start.11
  219.4 3.8 copy-start.1
  219.4 3.8 copy-start.8
  219.4 4.5 %copy-start.3 = (f32[2048,128]{1,0:T(8,128)S(1)}, f32[2048,128]{1,0:T(8,128)}, u32[]{:S(2)}) copy-start(f32[2048,128]{1,0:T(8,128)} %get-tuple-element.397) | copy-start | bytes 3145732 | tf_op jit(solution)/shard_map/while/body/eval_jaxpr/while
  224.0 2.0 copy-start.9
  225.0 1.0 copy-start.4
  226.6 123.5 %copy-start.6 = (bf16[16,128,512]{2,1,0:T(8,128)(2,1)S(1)}, bf16[16,128,512]{2,1,0:T(8,128)(2,1)}, u32[]{:S(2)}) copy-start(bf16[16,128,512]{2,1,0:T(8,128)(2,1)} %copy-done.5) | copy-start | bytes 6291460
  230.8 122.1 %copy-start.10 = (f32[2,128,4,128]{3,1,2,0:T(8,128)S(1)}, f32[2,128,4,128]{3,1,2,0:T(8,128)}, u32[]{:S(2)}) copy-start(f32[2,128,4,128]{3,1,2,0:T(8,128)} %get-tuple-element.111) | copy-start | bytes 1572868
  230.8 158.0 %all-gather.6.cloned.1.call-start = ((), (), s32[]{:S(2)}) async-start(), calls=%async_computation.3 | async-start | bytes 2621440 | tf_op jit(solution)/shard_map/all_gather | solution.py:11
Sparse Core Ops, SparseCore 0:
  10.7 44.6 all-gather.3
  230.9 119.1 all-reduce.2
  353.0 35.7 all-gather.5
